TPU v7x, 128 devices: a whole 4x4x4 slice. The times are simulated.
128 devices in a mesh: seq: 16 (over y, x_lo, core), head: 8 (over x_hi, z).
Axes of the slice: x: 4 (x_hi: 2, x_lo: 2; x = x_hi * 2 + x_lo), y: 4, z: 4, core: 2. Of those that a mesh axis runs over, the one named last changes fastest.
Arguments:
- queries: bfloat16 [8192, 8192], P('seq', 'head'), may hold values from -60 to 60
- keys: bfloat16 [8192, 1024], P('seq', 'head'), may hold values from -6 to 6
- values: bfloat16 [8192, 1024], P('seq', 'head'), may hold values from -6 to 6
- positions: int32 [8192], P('seq'), may hold values from 0 to 8191, as said below
- out_weight: bfloat16 [8192, 8192], P('head', 'seq'), may hold values from -0.25 to 0.25
Outputs:
- mixed: bfloat16 [8192, 8192], P('seq', 'head')
Inputs may be any that keep to these rules, and one draw needn't show every extreme that they name: positions is a permutation of the document's positions; each aligned group of 128 rows holds 128 consecutive positions in increasing order.
All inputs are finite; a program needn't handle non-finite values.
Results may differ from a plain program's by a relative error of at most 0.018.
Values may be sent and summed in bfloat16 or wider, within the bound.
No kernel may reach another device: no remote copies, remote signals or barrier semaphores. Data moves between devices by JAX's collectives and lax.ppermute only.
A program may use at most 128 MiB of HBM per device.

v0:
```python
import math

import jax
import jax.numpy as jnp
from jax import lax
from jax.sharding import PartitionSpec as P

HEADS = 64
KV_HEADS = 8
HD = 128


masked_score = -1e30


def shifted(block, axis, distance):
    devices = range(lax.axis_size(axis))
    route = [((i - distance) % len(devices), i) for i in devices]
    return lax.ppermute(block, axis, route)


def absorb_block(running, key_block, value_block, key_pos, query_heads, query_pos, top_query):
    count = key_block.shape[0]
    groups = query_heads.shape[1]
    scale = 1.0 / math.sqrt(query_heads.shape[3])

    def update(state):
        best_old, total_old, accum_old = state
        keys_split = key_block.reshape(count, groups, -1)
        values_split = value_block.reshape(count, groups, -1)
        scores = (
            jnp.einsum(
                "qgrd,kgd->grqk", query_heads, keys_split, preferred_element_type=jnp.float32
            )
            * scale
        )
        visible = key_pos[None, :] <= query_pos[:, None]
        scores = jnp.where(visible, scores, masked_score)
        best_new = jnp.maximum(best_old, jnp.max(scores, axis=-1))
        weights = jnp.where(visible, jnp.exp(scores - best_new[..., None]), 0.0)
        factor = jnp.exp(best_old - best_new)
        total_new = total_old * factor + jnp.sum(weights, axis=-1)
        accum_new = accum_old * factor[..., None] + jnp.einsum(
            "grqk,kgd->grqd",
            weights.astype(jnp.bfloat16),
            values_split,
            preferred_element_type=jnp.float32,
        )
        return (best_new, total_new, accum_new)

    return lax.cond(jnp.min(key_pos) > top_query, lambda state: state, update, running)


def per_device(queries, keys, values, positions, out_weight):
    row_count = queries.shape[0]
    ratio = HEADS // KV_HEADS
    groups = keys.shape[1] // HD
    all_positions = lax.all_gather(positions, "seq", axis=0, tiled=True)
    top_query = jnp.max(positions)
    query_heads = queries.reshape(row_count, groups, ratio, HD)
    kv_pair = jnp.stack([keys, values])

    def absorb_piece(running, pair_piece, start):
        count = pair_piece.shape[1]
        span = min(count, row_count)
        blocks = count // span

        def one_block(index, state):
            offset = (index * span).astype(jnp.int32)
            key_pos = lax.dynamic_slice_in_dim(all_positions, start + offset, span, 0)
            return absorb_block(
                state, pair_piece[0], pair_piece[1], key_pos, query_heads, positions, top_query
            )

        return lax.fori_loop(0, blocks, one_block, running)

    initial = (
        jnp.full((groups, ratio, row_count), masked_score, jnp.float32),
        jnp.zeros((groups, ratio, row_count), jnp.float32),
        jnp.zeros((groups, ratio, row_count, HD), jnp.float32),
    )
    seq_count = lax.axis_size("seq")
    own_index = lax.axis_index("seq")
    running = absorb_piece(initial, kv_pair, own_index * row_count)

    def cycle_step(step, carried):
        state, moving = carried
        moving = shifted(moving, "seq", 1)
        source = (own_index - step) % seq_count
        return (absorb_piece(state, moving, source * row_count), moving)

    running, kv_last = lax.fori_loop(1, seq_count, cycle_step, (running, kv_pair))
    best, total, accum = running
    attention = (accum / total[..., None]).astype(jnp.bfloat16)
    attention = jnp.transpose(attention, (2, 0, 1, 3)).reshape(row_count, groups * ratio * HD)
    terms = jnp.dot(
        attention,
        lax.all_gather(out_weight, "seq", axis=1, tiled=True),
        preferred_element_type=jnp.float32,
    ).astype(jnp.bfloat16)
    return (
        lax.psum_scatter(terms, "head", scatter_dimension=1, tiled=True)
        .astype(jnp.float32)
        .astype(jnp.bfloat16)
    )


def solution(mesh):
    placed = (P("seq", "head"), P("seq", "head"), P("seq", "head"), P("seq"), P("head", "seq"))
    return jax.shard_map(
        per_device, mesh=mesh, in_specs=placed, out_specs=P("seq", "head"), check_vma=False
    )
```

profile of v0, /device:TPU:25, one launch (start us, length us, event | category | flops | bytes accessed | tf_op | source)
XLA Modules:
  0.0 437.0 jit_solution(10718276367478677340)
XLA Ops:
  10.1 17.2 %all-gather = s32[16,1,512]{2,1,0:T(1,128)S(1)} all-gather(s32[1,1,512]{2,1,0:T(1,128)} %bitcast.113), channel_id=1, replica_groups=mesh['seq'=16,'head'=8] {'seq'}, dimensions={0}, use_global_device_ids=true | all-gather | bytes 34816 | tf_op jit(solution)/shard_map/all_gather | solution.py:58
  30.2 8.9 %conditional.2 = (f32[1,8,512]{2,1,0:T(8,128)S(1)}, f32[1,8,512]{2,1,0:T(8,128)S(1)}, f32[1,8,512,128]{3,2,1,0:T(8,128)S(1)}) conditional(s32[]{:T(128)} %convert_element_type.29, (s32[512]{0:T(512)S(1)}, s32[512]{0:T(512)}, bf16[512,1,8,128]{0,3,2,1:T(8,128)(2,1)S(1)}, bf16[512,128]{1,0:T(8,128)(2,1)}, f32[1,8,512]{2,1,0:T(8,128)S(1)}, ...), branch_computations={%region_2.5_spmd, %region_5.6_spmd} | conditional | flops 1102327808 | bytes 32477236 | solution.py:51
  31.1 2.5 fusion
  35.7 3.1 bitcast_add_fusion
  40.4 244.3 %while.28 = (s32[]{:T(128)}, f32[1,8,512]{2,1,0:T(8,128)S(1)}, f32[1,8,512]{2,1,0:T(8,128)S(1)}, f32[1,8,512,128]{3,2,1,0:T(8,128)}, bf16[2,512,128]{2,1,0:T(8,1...) while((s32[]{:T(128)}, f32[1,8,512]{2,1,0:T(8,128)S(1)}, ...), condition=%wide.region_12.0_spmd, body=%wide.region_6.12_spmd.sunk | while | flops 1102328320 | bytes 50340376 | solution.py:92
  42.5 7.0 %collective-permute-done = bf16[2,512,128]{2,1,0:T(8,128)(2,1)S(1)} collective-permute-done((bf16[2,512,128]{2,1,0:T(8,128)(2,1)S(1)}, bf16[2,512,128]{2,1,0:T(8,128)(2,1)S(1)}, u32[]{:S(2)}, u32[]{:S(2)}) %collective-permute-start) | collective-permute-done | bytes 262176 | tf_op jit(solution)/shard_map/while/body/eval_jaxpr/ppermute | solution.py:19
  49.6 7.8 %conditional.4 = (f32[1,8,512]{2,1,0:T(8,128)S(1)}, f32[1,8,512]{2,1,0:T(8,128)S(1)}, f32[1,8,512,128]{3,2,1,0:T(8,128)}) conditional(s32[]{:T(128)} %convert_element_type.47, (s32[512]{0:T(512)S(1)}, s32[512]{0:T(512)}, bf16[2,512,128]{2,1,0:T(8,128)(2,1)S(1)}, bf16[512,1,8,128]{3,0,2,1:T(8,128)(2,1)S(1)}, f32[1,8,512]{2,1,0:T(8,128)S(1)}, ...), branch_computations={%region_8.10_spmd, %region_11.11_spmd} | conditional | flops 1102327808 | bytes 48730192 | solution.py:51
  52.2 3.1 bitcast_add_fusion.2
  55.3 2.0 fusion.19
  57.4 2.6 collective-permute-start
  61.9 7.0 %collective-permute-done = bf16[2,512,128]{2,1,0:T(8,128)(2,1)S(1)} collective-permute-done((bf16[2,512,128]{2,1,0:T(8,128)(2,1)S(1)}, bf16[2,512,128]{2,1,0:T(8,128)(2,1)S(1)}, u32[]{:S(2)}, u32[]{:S(2)}) %collective-permute-start) | collective-permute-done | bytes 262176 | tf_op jit(solution)/shard_map/while/body/eval_jaxpr/ppermute | solution.py:19
  68.9 7.8 %conditional.4 = (f32[1,8,512]{2,1,0:T(8,128)S(1)}, f32[1,8,512]{2,1,0:T(8,128)S(1)}, f32[1,8,512,128]{3,2,1,0:T(8,128)}) conditional(s32[]{:T(128)} %convert_element_type.47, (s32[512]{0:T(512)S(1)}, s32[512]{0:T(512)}, bf16[2,512,128]{2,1,0:T(8,128)(2,1)S(1)}, bf16[512,1,8,128]{3,0,2,1:T(8,128)(2,1)S(1)}, f32[1,8,512]{2,1,0:T(8,128)S(1)}, ...), branch_computations={%region_8.10_spmd, %region_11.11_spmd} | conditional | flops 1102327808 | bytes 48730192 | solution.py:51
  71.5 3.1 bitcast_add_fusion.2
  74.6 2.0 fusion.19
  76.8 2.6 collective-permute-start
  81.2 7.0 %collective-permute-done = bf16[2,512,128]{2,1,0:T(8,128)(2,1)S(1)} collective-permute-done((bf16[2,512,128]{2,1,0:T(8,128)(2,1)S(1)}, bf16[2,512,128]{2,1,0:T(8,128)(2,1)S(1)}, u32[]{:S(2)}, u32[]{:S(2)}) %collective-permute-start) | collective-permute-done | bytes 262176 | tf_op jit(solution)/shard_map/while/body/eval_jaxpr/ppermute | solution.py:19
  88.2 7.8 %conditional.4 = (f32[1,8,512]{2,1,0:T(8,128)S(1)}, f32[1,8,512]{2,1,0:T(8,128)S(1)}, f32[1,8,512,128]{3,2,1,0:T(8,128)}) conditional(s32[]{:T(128)} %convert_element_type.47, (s32[512]{0:T(512)S(1)}, s32[512]{0:T(512)}, bf16[2,512,128]{2,1,0:T(8,128)(2,1)S(1)}, bf16[512,1,8,128]{3,0,2,1:T(8,128)(2,1)S(1)}, f32[1,8,512]{2,1,0:T(8,128)S(1)}, ...), branch_computations={%region_8.10_spmd, %region_11.11_spmd} | conditional | flops 1102327808 | bytes 48730192 | solution.py:51
  90.8 3.1 bitcast_add_fusion.2
  94.0 2.0 fusion.19
  96.1 2.5 collective-permute-start
  100.5 7.0 %collective-permute-done = bf16[2,512,128]{2,1,0:T(8,128)(2,1)S(1)} collective-permute-done((bf16[2,512,128]{2,1,0:T(8,128)(2,1)S(1)}, bf16[2,512,128]{2,1,0:T(8,128)(2,1)S(1)}, u32[]{:S(2)}, u32[]{:S(2)}) %collective-permute-start) | collective-permute-done | bytes 262176 | tf_op jit(solution)/shard_map/while/body/eval_jaxpr/ppermute | solution.py:19
  107.6 7.8 %conditional.4 = (f32[1,8,512]{2,1,0:T(8,128)S(1)}, f32[1,8,512]{2,1,0:T(8,128)S(1)}, f32[1,8,512,128]{3,2,1,0:T(8,128)}) conditional(s32[]{:T(128)} %convert_element_type.47, (s32[512]{0:T(512)S(1)}, s32[512]{0:T(512)}, bf16[2,512,128]{2,1,0:T(8,128)(2,1)S(1)}, bf16[512,1,8,128]{3,0,2,1:T(8,128)(2,1)S(1)}, f32[1,8,512]{2,1,0:T(8,128)S(1)}, ...), branch_computations={%region_8.10_spmd, %region_11.11_spmd} | conditional | flops 1102327808 | bytes 48730192 | solution.py:51
  110.2 3.1 bitcast_add_fusion.2
  113.3 2.0 fusion.19
  115.4 2.5 collective-permute-start
  121.3 7.8 %conditional.4 = (f32[1,8,512]{2,1,0:T(8,128)S(1)}, f32[1,8,512]{2,1,0:T(8,128)S(1)}, f32[1,8,512,128]{3,2,1,0:T(8,128)}) conditional(s32[]{:T(128)} %convert_element_type.47, (s32[512]{0:T(512)S(1)}, s32[512]{0:T(512)}, bf16[2,512,128]{2,1,0:T(8,128)(2,1)S(1)}, bf16[512,1,8,128]{3,0,2,1:T(8,128)(2,1)S(1)}, f32[1,8,512]{2,1,0:T(8,128)S(1)}, ...), branch_computations={%region_8.10_spmd, %region_11.11_spmd} | conditional | flops 1102327808 | bytes 48730192 | solution.py:51
  123.9 3.1 bitcast_add_fusion.2
  127.0 2.0 fusion.19
  129.2 2.5 collective-permute-start
  135.0 7.8 %conditional.4 = (f32[1,8,512]{2,1,0:T(8,128)S(1)}, f32[1,8,512]{2,1,0:T(8,128)S(1)}, f32[1,8,512,128]{3,2,1,0:T(8,128)}) conditional(s32[]{:T(128)} %convert_element_type.47, (s32[512]{0:T(512)S(1)}, s32[512]{0:T(512)}, bf16[2,512,128]{2,1,0:T(8,128)(2,1)S(1)}, bf16[512,1,8,128]{3,0,2,1:T(8,128)(2,1)S(1)}, f32[1,8,512]{2,1,0:T(8,128)S(1)}, ...), branch_computations={%region_8.10_spmd, %region_11.11_spmd} | conditional | flops 1102327808 | bytes 48730192 | solution.py:51
  137.6 3.1 bitcast_add_fusion.2
  140.8 2.0 fusion.19
  142.9 3.9 collective-permute-start
  150.1 7.8 %conditional.4 = (f32[1,8,512]{2,1,0:T(8,128)S(1)}, f32[1,8,512]{2,1,0:T(8,128)S(1)}, f32[1,8,512,128]{3,2,1,0:T(8,128)}) conditional(s32[]{:T(128)} %convert_element_type.47, (s32[512]{0:T(512)S(1)}, s32[512]{0:T(512)}, bf16[2,512,128]{2,1,0:T(8,128)(2,1)S(1)}, bf16[512,1,8,128]{3,0,2,1:T(8,128)(2,1)S(1)}, f32[1,8,512]{2,1,0:T(8,128)S(1)}, ...), branch_computations={%region_8.10_spmd, %region_11.11_spmd} | conditional | flops 1102327808 | bytes 48730192 | solution.py:51
  152.7 3.1 bitcast_add_fusion.2
  155.8 2.0 fusion.19
  157.9 4.7 %collective-permute-start = (bf16[2,512,128]{2,1,0:T(8,128)(2,1)S(1)}, bf16[2,512,128]{2,1,0:T(8,128)(2,1)S(1)}, u32[]{:S(2)}, u32[]{:S(2)}) collective-permute-start(bf16[2,512,128]{2,1,0:T(8,128)(2,1)S(1)} %get-tuple-element.597), channel_id=1, source_target_pairs={{120,0},{0,8},{8,16},{16,24},{24,32},{32,40},{40,48},{48,56},{56,6... | collective-permute-start | bytes 786440 | tf_op jit(solution)/shard_map/while/body/eval_jaxpr/ppermute | solution.py:19
  165.9 7.8 %conditional.4 = (f32[1,8,512]{2,1,0:T(8,128)S(1)}, f32[1,8,512]{2,1,0:T(8,128)S(1)}, f32[1,8,512,128]{3,2,1,0:T(8,128)}) conditional(s32[]{:T(128)} %convert_element_type.47, (s32[512]{0:T(512)S(1)}, s32[512]{0:T(512)}, bf16[2,512,128]{2,1,0:T(8,128)(2,1)S(1)}, bf16[512,1,8,128]{3,0,2,1:T(8,128)(2,1)S(1)}, f32[1,8,512]{2,1,0:T(8,128)S(1)}, ...), branch_computations={%region_8.10_spmd, %region_11.11_spmd} | conditional | flops 1102327808 | bytes 48730192 | solution.py:51
  168.5 3.1 bitcast_add_fusion.2
  171.6 2.0 fusion.19
  173.8 4.7 %collective-permute-start = (bf16[2,512,128]{2,1,0:T(8,128)(2,1)S(1)}, bf16[2,512,128]{2,1,0:T(8,128)(2,1)S(1)}, u32[]{:S(2)}, u32[]{:S(2)}) collective-permute-start(bf16[2,512,128]{2,1,0:T(8,128)(2,1)S(1)} %get-tuple-element.597), channel_id=1, source_target_pairs={{120,0},{0,8},{8,16},{16,24},{24,32},{32,40},{40,48},{48,56},{56,6... | collective-permute-start | bytes 786440 | tf_op jit(solution)/shard_map/while/body/eval_jaxpr/ppermute | solution.py:19
  181.8 7.8 %conditional.4 = (f32[1,8,512]{2,1,0:T(8,128)S(1)}, f32[1,8,512]{2,1,0:T(8,128)S(1)}, f32[1,8,512,128]{3,2,1,0:T(8,128)}) conditional(s32[]{:T(128)} %convert_element_type.47, (s32[512]{0:T(512)S(1)}, s32[512]{0:T(512)}, bf16[2,512,128]{2,1,0:T(8,128)(2,1)S(1)}, bf16[512,1,8,128]{3,0,2,1:T(8,128)(2,1)S(1)}, f32[1,8,512]{2,1,0:T(8,128)S(1)}, ...), branch_computations={%region_8.10_spmd, %region_11.11_spmd} | conditional | flops 1102327808 | bytes 48730192 | solution.py:51
  184.4 3.1 bitcast_add_fusion.2
  189.6 4.7 %collective-permute-start = (bf16[2,512,128]{2,1,0:T(8,128)(2,1)S(1)}, bf16[2,512,128]{2,1,0:T(8,128)(2,1)S(1)}, u32[]{:S(2)}, u32[]{:S(2)}) collective-permute-start(bf16[2,512,128]{2,1,0:T(8,128)(2,1)S(1)} %get-tuple-element.597), channel_id=1, source_target_pairs={{120,0},{0,8},{8,16},{16,24},{24,32},{32,40},{40,48},{48,56},{56,6... | collective-permute-start | bytes 786440 | tf_op jit(solution)/shard_map/while/body/eval_jaxpr/ppermute | solution.py:19
  197.6 7.8 %conditional.4 = (f32[1,8,512]{2,1,0:T(8,128)S(1)}, f32[1,8,512]{2,1,0:T(8,128)S(1)}, f32[1,8,512,128]{3,2,1,0:T(8,128)}) conditional(s32[]{:T(128)} %convert_element_type.47, (s32[512]{0:T(512)S(1)}, s32[512]{0:T(512)}, bf16[2,512,128]{2,1,0:T(8,128)(2,1)S(1)}, bf16[512,1,8,128]{3,0,2,1:T(8,128)(2,1)S(1)}, f32[1,8,512]{2,1,0:T(8,128)S(1)}, ...), branch_computations={%region_8.10_spmd, %region_11.11_spmd} | conditional | flops 1102327808 | bytes 48730192 | solution.py:51
  200.2 3.1 bitcast_add_fusion.2
  205.5 4.7 %collective-permute-start = (bf16[2,512,128]{2,1,0:T(8,128)(2,1)S(1)}, bf16[2,512,128]{2,1,0:T(8,128)(2,1)S(1)}, u32[]{:S(2)}, u32[]{:S(2)}) collective-permute-start(bf16[2,512,128]{2,1,0:T(8,128)(2,1)S(1)} %get-tuple-element.597), channel_id=1, source_target_pairs={{120,0},{0,8},{8,16},{16,24},{24,32},{32,40},{40,48},{48,56},{56,6... | collective-permute-start | bytes 786440 | tf_op jit(solution)/shard_map/while/body/eval_jaxpr/ppermute | solution.py:19
  213.4 7.8 %conditional.4 = (f32[1,8,512]{2,1,0:T(8,128)S(1)}, f32[1,8,512]{2,1,0:T(8,128)S(1)}, f32[1,8,512,128]{3,2,1,0:T(8,128)}) conditional(s32[]{:T(128)} %convert_element_type.47, (s32[512]{0:T(512)S(1)}, s32[512]{0:T(512)}, bf16[2,512,128]{2,1,0:T(8,128)(2,1)S(1)}, bf16[512,1,8,128]{3,0,2,1:T(8,128)(2,1)S(1)}, f32[1,8,512]{2,1,0:T(8,128)S(1)}, ...), branch_computations={%region_8.10_spmd, %region_11.11_spmd} | conditional | flops 1102327808 | bytes 48730192 | solution.py:51
  216.0 3.1 bitcast_add_fusion.2
  221.3 4.7 %collective-permute-start = (bf16[2,512,128]{2,1,0:T(8,128)(2,1)S(1)}, bf16[2,512,128]{2,1,0:T(8,128)(2,1)S(1)}, u32[]{:S(2)}, u32[]{:S(2)}) collective-permute-start(bf16[2,512,128]{2,1,0:T(8,128)(2,1)S(1)} %get-tuple-element.597), channel_id=1, source_target_pairs={{120,0},{0,8},{8,16},{16,24},{24,32},{32,40},{40,48},{48,56},{56,6... | collective-permute-start | bytes 786440 | tf_op jit(solution)/shard_map/while/body/eval_jaxpr/ppermute | solution.py:19
  229.3 7.8 %conditional.4 = (f32[1,8,512]{2,1,0:T(8,128)S(1)}, f32[1,8,512]{2,1,0:T(8,128)S(1)}, f32[1,8,512,128]{3,2,1,0:T(8,128)}) conditional(s32[]{:T(128)} %convert_element_type.47, (s32[512]{0:T(512)S(1)}, s32[512]{0:T(512)}, bf16[2,512,128]{2,1,0:T(8,128)(2,1)S(1)}, bf16[512,1,8,128]{3,0,2,1:T(8,128)(2,1)S(1)}, f32[1,8,512]{2,1,0:T(8,128)S(1)}, ...), branch_computations={%region_8.10_spmd, %region_11.11_spmd} | conditional | flops 1102327808 | bytes 48730192 | solution.py:51
  231.9 3.1 bitcast_add_fusion.2
  237.2 4.7 %collective-permute-start = (bf16[2,512,128]{2,1,0:T(8,128)(2,1)S(1)}, bf16[2,512,128]{2,1,0:T(8,128)(2,1)S(1)}, u32[]{:S(2)}, u32[]{:S(2)}) collective-permute-start(bf16[2,512,128]{2,1,0:T(8,128)(2,1)S(1)} %get-tuple-element.597), channel_id=1, source_target_pairs={{120,0},{0,8},{8,16},{16,24},{24,32},{32,40},{40,48},{48,56},{56,6... | collective-permute-start | bytes 786440 | tf_op jit(solution)/shard_map/while/body/eval_jaxpr/ppermute | solution.py:19
  245.1 7.8 %conditional.4 = (f32[1,8,512]{2,1,0:T(8,128)S(1)}, f32[1,8,512]{2,1,0:T(8,128)S(1)}, f32[1,8,512,128]{3,2,1,0:T(8,128)}) conditional(s32[]{:T(128)} %convert_element_type.47, (s32[512]{0:T(512)S(1)}, s32[512]{0:T(512)}, bf16[2,512,128]{2,1,0:T(8,128)(2,1)S(1)}, bf16[512,1,8,128]{3,0,2,1:T(8,128)(2,1)S(1)}, f32[1,8,512]{2,1,0:T(8,128)S(1)}, ...), branch_computations={%region_8.10_spmd, %region_11.11_spmd} | conditional | flops 1102327808 | bytes 48730192 | solution.py:51
  247.7 3.1 bitcast_add_fusion.2
  253.0 4.7 %collective-permute-start = (bf16[2,512,128]{2,1,0:T(8,128)(2,1)S(1)}, bf16[2,512,128]{2,1,0:T(8,128)(2,1)S(1)}, u32[]{:S(2)}, u32[]{:S(2)}) collective-permute-start(bf16[2,512,128]{2,1,0:T(8,128)(2,1)S(1)} %get-tuple-element.597), channel_id=1, source_target_pairs={{120,0},{0,8},{8,16},{16,24},{24,32},{32,40},{40,48},{48,56},{56,6... | collective-permute-start | bytes 786440 | tf_op jit(solution)/shard_map/while/body/eval_jaxpr/ppermute | solution.py:19
  261.0 7.8 %conditional.4 = (f32[1,8,512]{2,1,0:T(8,128)S(1)}, f32[1,8,512]{2,1,0:T(8,128)S(1)}, f32[1,8,512,128]{3,2,1,0:T(8,128)}) conditional(s32[]{:T(128)} %convert_element_type.47, (s32[512]{0:T(512)S(1)}, s32[512]{0:T(512)}, bf16[2,512,128]{2,1,0:T(8,128)(2,1)S(1)}, bf16[512,1,8,128]{3,0,2,1:T(8,128)(2,1)S(1)}, f32[1,8,512]{2,1,0:T(8,128)S(1)}, ...), branch_computations={%region_8.10_spmd, %region_11.11_spmd} | conditional | flops 1102327808 | bytes 48730192 | solution.py:51
  263.6 3.1 bitcast_add_fusion.2
  268.8 4.7 %collective-permute-start = (bf16[2,512,128]{2,1,0:T(8,128)(2,1)S(1)}, bf16[2,512,128]{2,1,0:T(8,128)(2,1)S(1)}, u32[]{:S(2)}, u32[]{:S(2)}) collective-permute-start(bf16[2,512,128]{2,1,0:T(8,128)(2,1)S(1)} %get-tuple-element.597), channel_id=1, source_target_pairs={{120,0},{0,8},{8,16},{16,24},{24,32},{32,40},{40,48},{48,56},{56,6... | collective-permute-start | bytes 786440 | tf_op jit(solution)/shard_map/while/body/eval_jaxpr/ppermute | solution.py:19
  276.8 7.8 %conditional.4 = (f32[1,8,512]{2,1,0:T(8,128)S(1)}, f32[1,8,512]{2,1,0:T(8,128)S(1)}, f32[1,8,512,128]{3,2,1,0:T(8,128)}) conditional(s32[]{:T(128)} %convert_element_type.47, (s32[512]{0:T(512)S(1)}, s32[512]{0:T(512)}, bf16[2,512,128]{2,1,0:T(8,128)(2,1)S(1)}, bf16[512,1,8,128]{3,0,2,1:T(8,128)(2,1)S(1)}, f32[1,8,512]{2,1,0:T(8,128)S(1)}, ...), branch_computations={%region_8.10_spmd, %region_11.11_spmd} | conditional | flops 1102327808 | bytes 48730192 | solution.py:51
  279.4 3.1 bitcast_add_fusion.2
  282.6 2.0 fusion.19
  286.9 17.0 %convolution_convert_fusion = bf16[512,8192]{1,0:T(8,128)(2,1)} fusion(bf16[512,1024]{0,1:T(8,128)(2,1)S(1)} %bitcast.111, bf16[1024,8192]{1,0:T(8,128)(2,1)} %all-gather.3.cloned.1.call-done), kind=kOutput, calls=%fused_computation.44 | convolution fusion | flops 8594128896 | bytes 26214400 | tf_op jit(solution)/shard_map/dot_general | solution.py:96
  303.9 126.3 %reduce-scatter.2.cloned.1.call-done = bf16[512,1024]{1,0:T(8,128)(2,1)} async-done(((bf16[512,8192]{1,0:T(8,128)(2,1)}), bf16[512,1024]{1,0:T(8,128)(2,1)}) %reduce-scatter.2.cloned.1.call-update) | async-done | bytes 1048592 | tf_op jit(solution)/shard_map/reduce_scatter | solution.py:102
  (206 shorter events, 89.6 us)
Async XLA Ops:
  6.5 280.4 %all-gather.3.cloned.1.call-start = ((), (), s32[]{:S(2)}) async-start(), calls=%async_computation.1 | async-start | bytes 17825792 | tf_op jit(solution)/shard_map/all_gather | solution.py:98
  7.3 422.9 %reduce-scatter.2.cloned.1.call-start = ((), (), s32[]{:S(2)}) async-start(), calls=%async_computation.2 | async-start | bytes 9437184 | tf_op jit(solution)/shard_map/reduce_scatter | solution.py:102
  31.1 4.6 %copy-start.3 = (bf16[512,128]{1,0:T(8,128)(2,1)S(1)}, bf16[512,128]{1,0:T(8,128)(2,1)}, u32[]{:S(2)}) copy-start(bf16[512,128]{1,0:T(8,128)(2,1)} %get-tuple-element.394) | copy-start | bytes 393220 | tf_op jit(solution)/shard_map/while/body/eval_jaxpr/cond
  39.1 1.3 copy-start
  40.4 9.2 %collective-permute-start = (bf16[2,512,128]{2,1,0:T(8,128)(2,1)S(1)}, bf16[2,512,128]{2,1,0:T(8,128)(2,1)S(1)}, u32[]{:S(2)}, u32[]{:S(2)}) collective-permute-start(bf16[2,512,128]{2,1,0:T(8,128)(2,1)S(1)} %get-tuple-element.597), channel_id=1, source_target_pairs={{120,0},{0,8},{8,16},{16,24},{24,32},{32,40},{40,48},{48,56},{56,6... | collective-permute-start | bytes 786440 | tf_op jit(solution)/shard_map/while/body/eval_jaxpr/ppermute | solution.py:19
  49.6 2.6 copy-start.1
  55.3 2.1 copy-start.2
  57.4 11.5 %collective-permute-start = (bf16[2,512,128]{2,1,0:T(8,128)(2,1)S(1)}, bf16[2,512,128]{2,1,0:T(8,128)(2,1)S(1)}, u32[]{:S(2)}, u32[]{:S(2)}) collective-permute-start(bf16[2,512,128]{2,1,0:T(8,128)(2,1)S(1)} %get-tuple-element.597), channel_id=1, source_target_pairs={{120,0},{0,8},{8,16},{16,24},{24,32},{32,40},{40,48},{48,56},{56,6... | collective-permute-start | bytes 786440 | tf_op jit(solution)/shard_map/while/body/eval_jaxpr/ppermute | solution.py:19
  68.9 2.6 copy-start.1
  74.6 2.1 copy-start.2
  76.8 11.5 %collective-permute-start = (bf16[2,512,128]{2,1,0:T(8,128)(2,1)S(1)}, bf16[2,512,128]{2,1,0:T(8,128)(2,1)S(1)}, u32[]{:S(2)}, u32[]{:S(2)}) collective-permute-start(bf16[2,512,128]{2,1,0:T(8,128)(2,1)S(1)} %get-tuple-element.597), channel_id=1, source_target_pairs={{120,0},{0,8},{8,16},{16,24},{24,32},{32,40},{40,48},{48,56},{56,6... | collective-permute-start | bytes 786440 | tf_op jit(solution)/shard_map/while/body/eval_jaxpr/ppermute | solution.py:19
  88.2 2.6 copy-start.1
  94.0 2.1 copy-start.2
  96.1 11.5 %collective-permute-start = (bf16[2,512,128]{2,1,0:T(8,128)(2,1)S(1)}, bf16[2,512,128]{2,1,0:T(8,128)(2,1)S(1)}, u32[]{:S(2)}, u32[]{:S(2)}) collective-permute-start(bf16[2,512,128]{2,1,0:T(8,128)(2,1)S(1)} %get-tuple-element.597), channel_id=1, source_target_pairs={{120,0},{0,8},{8,16},{16,24},{24,32},{32,40},{40,48},{48,56},{56,6... | collective-permute-start | bytes 786440 | tf_op jit(solution)/shard_map/while/body/eval_jaxpr/ppermute | solution.py:19
  107.6 2.6 copy-start.1
  113.3 2.1 copy-start.2
  115.4 5.9 %collective-permute-start = (bf16[2,512,128]{2,1,0:T(8,128)(2,1)S(1)}, bf16[2,512,128]{2,1,0:T(8,128)(2,1)S(1)}, u32[]{:S(2)}, u32[]{:S(2)}) collective-permute-start(bf16[2,512,128]{2,1,0:T(8,128)(2,1)S(1)} %get-tuple-element.597), channel_id=1, source_target_pairs={{120,0},{0,8},{8,16},{16,24},{24,32},{32,40},{40,48},{48,56},{56,6... | collective-permute-start | bytes 786440 | tf_op jit(solution)/shard_map/while/body/eval_jaxpr/ppermute | solution.py:19
  121.3 2.6 copy-start.1
  127.0 2.1 copy-start.2
  129.2 5.9 %collective-permute-start = (bf16[2,512,128]{2,1,0:T(8,128)(2,1)S(1)}, bf16[2,512,128]{2,1,0:T(8,128)(2,1)S(1)}, u32[]{:S(2)}, u32[]{:S(2)}) collective-permute-start(bf16[2,512,128]{2,1,0:T(8,128)(2,1)S(1)} %get-tuple-element.597), channel_id=1, source_target_pairs={{120,0},{0,8},{8,16},{16,24},{24,32},{32,40},{40,48},{48,56},{56,6... | collective-permute-start | bytes 786440 | tf_op jit(solution)/shard_map/while/body/eval_jaxpr/ppermute | solution.py:19
  135.0 2.6 copy-start.1
  140.7 2.1 copy-start.2
  142.9 7.2 %collective-permute-start = (bf16[2,512,128]{2,1,0:T(8,128)(2,1)S(1)}, bf16[2,512,128]{2,1,0:T(8,128)(2,1)S(1)}, u32[]{:S(2)}, u32[]{:S(2)}) collective-permute-start(bf16[2,512,128]{2,1,0:T(8,128)(2,1)S(1)} %get-tuple-element.597), channel_id=1, source_target_pairs={{120,0},{0,8},{8,16},{16,24},{24,32},{32,40},{40,48},{48,56},{56,6... | collective-permute-start | bytes 786440 | tf_op jit(solution)/shard_map/while/body/eval_jaxpr/ppermute | solution.py:19
  150.1 2.6 copy-start.1
  155.8 2.1 copy-start.2
  157.9 8.0 %collective-permute-start = (bf16[2,512,128]{2,1,0:T(8,128)(2,1)S(1)}, bf16[2,512,128]{2,1,0:T(8,128)(2,1)S(1)}, u32[]{:S(2)}, u32[]{:S(2)}) collective-permute-start(bf16[2,512,128]{2,1,0:T(8,128)(2,1)S(1)} %get-tuple-element.597), channel_id=1, source_target_pairs={{120,0},{0,8},{8,16},{16,24},{24,32},{32,40},{40,48},{48,56},{56,6... | collective-permute-start | bytes 786440 | tf_op jit(solution)/shard_map/while/body/eval_jaxpr/ppermute | solution.py:19
  165.9 2.6 copy-start.1
  171.6 2.1 copy-start.2
  173.8 8.0 %collective-permute-start = (bf16[2,512,128]{2,1,0:T(8,128)(2,1)S(1)}, bf16[2,512,128]{2,1,0:T(8,128)(2,1)S(1)}, u32[]{:S(2)}, u32[]{:S(2)}) collective-permute-start(bf16[2,512,128]{2,1,0:T(8,128)(2,1)S(1)} %get-tuple-element.597), channel_id=1, source_target_pairs={{120,0},{0,8},{8,16},{16,24},{24,32},{32,40},{40,48},{48,56},{56,6... | collective-permute-start | bytes 786440 | tf_op jit(solution)/shard_map/while/body/eval_jaxpr/ppermute | solution.py:19
  181.8 2.6 copy-start.1
  187.5 2.1 copy-start.2
  189.6 8.0 %collective-permute-start = (bf16[2,512,128]{2,1,0:T(8,128)(2,1)S(1)}, bf16[2,512,128]{2,1,0:T(8,128)(2,1)S(1)}, u32[]{:S(2)}, u32[]{:S(2)}) collective-permute-start(bf16[2,512,128]{2,1,0:T(8,128)(2,1)S(1)} %get-tuple-element.597), channel_id=1, source_target_pairs={{120,0},{0,8},{8,16},{16,24},{24,32},{32,40},{40,48},{48,56},{56,6... | collective-permute-start | bytes 786440 | tf_op jit(solution)/shard_map/while/body/eval_jaxpr/ppermute | solution.py:19
  197.6 2.6 copy-start.1
  203.3 2.1 copy-start.2
  205.5 8.0 %collective-permute-start = (bf16[2,512,128]{2,1,0:T(8,128)(2,1)S(1)}, bf16[2,512,128]{2,1,0:T(8,128)(2,1)S(1)}, u32[]{:S(2)}, u32[]{:S(2)}) collective-permute-start(bf16[2,512,128]{2,1,0:T(8,128)(2,1)S(1)} %get-tuple-element.597), channel_id=1, source_target_pairs={{120,0},{0,8},{8,16},{16,24},{24,32},{32,40},{40,48},{48,56},{56,6... | collective-permute-start | bytes 786440 | tf_op jit(solution)/shard_map/while/body/eval_jaxpr/ppermute | solution.py:19
  213.4 2.6 copy-start.1
  219.2 2.1 copy-start.2
  221.3 8.0 %collective-permute-start = (bf16[2,512,128]{2,1,0:T(8,128)(2,1)S(1)}, bf16[2,512,128]{2,1,0:T(8,128)(2,1)S(1)}, u32[]{:S(2)}, u32[]{:S(2)}) collective-permute-start(bf16[2,512,128]{2,1,0:T(8,128)(2,1)S(1)} %get-tuple-element.597), channel_id=1, source_target_pairs={{120,0},{0,8},{8,16},{16,24},{24,32},{32,40},{40,48},{48,56},{56,6... | collective-permute-start | bytes 786440 | tf_op jit(solution)/shard_map/while/body/eval_jaxpr/ppermute | solution.py:19
  229.3 2.6 copy-start.1
  235.0 2.1 copy-start.2
  237.2 8.0 %collective-permute-start = (bf16[2,512,128]{2,1,0:T(8,128)(2,1)S(1)}, bf16[2,512,128]{2,1,0:T(8,128)(2,1)S(1)}, u32[]{:S(2)}, u32[]{:S(2)}) collective-permute-start(bf16[2,512,128]{2,1,0:T(8,128)(2,1)S(1)} %get-tuple-element.597), channel_id=1, source_target_pairs={{120,0},{0,8},{8,16},{16,24},{24,32},{32,40},{40,48},{48,56},{56,6... | collective-permute-start | bytes 786440 | tf_op jit(solution)/shard_map/while/body/eval_jaxpr/ppermute | solution.py:19
  245.1 2.6 copy-start.1
  250.9 2.1 copy-start.2
  253.0 8.0 %collective-permute-start = (bf16[2,512,128]{2,1,0:T(8,128)(2,1)S(1)}, bf16[2,512,128]{2,1,0:T(8,128)(2,1)S(1)}, u32[]{:S(2)}, u32[]{:S(2)}) collective-permute-start(bf16[2,512,128]{2,1,0:T(8,128)(2,1)S(1)} %get-tuple-element.597), channel_id=1, source_target_pairs={{120,0},{0,8},{8,16},{16,24},{24,32},{32,40},{40,48},{48,56},{56,6... | collective-permute-start | bytes 786440 | tf_op jit(solution)/shard_map/while/body/eval_jaxpr/ppermute | solution.py:19
  261.0 2.6 copy-start.1
  266.7 2.1 copy-start.2
  268.8 8.0 %collective-permute-start = (bf16[2,512,128]{2,1,0:T(8,128)(2,1)S(1)}, bf16[2,512,128]{2,1,0:T(8,128)(2,1)S(1)}, u32[]{:S(2)}, u32[]{:S(2)}) collective-permute-start(bf16[2,512,128]{2,1,0:T(8,128)(2,1)S(1)} %get-tuple-element.597), channel_id=1, source_target_pairs={{120,0},{0,8},{8,16},{16,24},{24,32},{32,40},{40,48},{48,56},{56,6... | collective-permute-start | bytes 786440 | tf_op jit(solution)/shard_map/while/body/eval_jaxpr/ppermute | solution.py:19
  276.8 2.6 copy-start.1
  282.5 2.1 copy-start.2
Sparse Core Ops, SparseCore 0:
  9.0 107.3 all-gather.2
  304.0 126.0 reduce-scatter.1
where the time goes:
time: 439 us; the launch traced here: 437 us
  waiting for transfers between devices  171 us (39%)
  matrix products  91.9 us (21%)
  other arithmetic  63.7 us (15%)
  starting transfers between devices  54.2 us (12%)
  loops' own time  19.5 us (4%)
  blocking collectives  17.2 us (4%)
  between operations  14.7 us (3%)
  local copies, waits for them, and re-layouts  4.71 us (1%)
    reduce_scatter x1, waiting for transfers between devices, per_device(): lax.psum_scatter(terms, 'head', scatter_dimension=1, tiled=True)  126 us
    ppermute x15, starting transfers between devices, shifted(): return lax.ppermute(block, axis, route)  54.1 us
    dot_general x16, matrix products, update(): jnp.einsum('grqk,kgd->grqd', weights.astype(jnp.bfloat16), values_split,...  49.9 us
    ppermute x15, waiting for transfers between devices, shifted(): return lax.ppermute(block, axis, route)  43.9 us
    reduce_sum x16, other arithmetic, update(): total_new = total_old * factor + jnp.sum(weights, axis=-1)  32.5 us
    dot_general x16, matrix products, update(): jnp.einsum('qgrd,kgd->grqk', query_heads, keys_split, preferred_element_t...  25.1 us
    another operation x1, loops' own time, per_device(): lax.fori_loop(1, seq_count, cycle_step, (running, kv_pair))  18.1 us
    all_gather x1, blocking collectives, per_device(): all_positions = lax.all_gather(positions, 'seq', axis=0, tiled=True)  17.2 us
  transfers between devices with their start and end apart: 17, of which 16 were waited for; matrix products, arithmetic and copies ran while one was open for 33% of the time, Pallas kernels for 0%

commit v1 on v0

v1 whole, which is shorter than its diff:
```python
import functools
import math

import jax
import jax.numpy as jnp
from jax import lax
from jax.experimental import pallas as pl
from jax.experimental.pallas import tpu as pltpu
from jax.sharding import Mesh
from jax.sharding import PartitionSpec as P

HD = 128
BLK = 128
TILE = 512
AXES = ("y", "xl", "c", "xh", "z")
SIZES = {"y": 4, "xl": 2, "c": 2, "xh": 2, "z": 4}
masked_score = -1e30
VMEM_BYTES = 56 << 20


def move(block, axes, target):
    sizes = [SIZES[a] for a in axes]
    count = math.prod(sizes)
    route = []
    for i in range(count):
        rest, at = i, []
        for size in reversed(sizes):
            at.append(rest % size)
            rest //= size
        to = target(*reversed(at))
        j = 0
        for t, size in zip(to, sizes):
            j = j * size + t % size
        route.append((i, j))
    return lax.ppermute(block, axes, route)


def sort_blocks(slot_ref, *refs):
    sources, (keys_ref, values_ref, sem) = refs[:16], refs[16:]
    copies = []
    for r in range(16):
        for b in range(4):
            slot = pl.multiple_of(slot_ref[r * 4 + b] * BLK, BLK)
            for part, sorted_ref in enumerate((keys_ref, values_ref)):
                copies.append(
                    pltpu.make_async_copy(
                        sources[r].at[pl.ds(part * 512 + b * BLK, BLK), :],
                        sorted_ref.at[pl.ds(slot, BLK), :],
                        sem.at[part, r * 4 + b],
                    )
                )
    for copy in copies:
        copy.start()
    for copy in copies:
        copy.wait()


def sorted_kv(slots, sources):
    anywhere = pl.BlockSpec(memory_space=pl.ANY)
    inside = pl.BlockSpec(memory_space=pltpu.VMEM)
    sorted_shape = jax.ShapeDtypeStruct((64 * BLK, HD), jnp.bfloat16)
    return pl.pallas_call(
        sort_blocks,
        out_shape=(sorted_shape, sorted_shape),
        in_specs=[pl.BlockSpec(memory_space=pltpu.SMEM)] + [anywhere] * 16,
        out_specs=(inside, inside),
        scratch_shapes=[pltpu.SemaphoreType.DMA((2, 64))],
        cost_estimate=pl.CostEstimate(flops=0, bytes_accessed=8 << 20, transcendentals=0),
        name="sort_blocks",
    )(slots, *sources)


def attend(chunk, own_ref, q_ref, keys_ref, values_ref, out_ref, k_s, v_s, q_s, s_s, acc, best, total, sem):
    rows = 8 * BLK
    factor = math.log2(math.e) / math.sqrt(HD)
    block = own_ref[chunk]
    tiles = block // (TILE // BLK) + 1

    def copies(j):
        at = pl.multiple_of(j * TILE, TILE)
        return (
            pltpu.make_async_copy(
                keys_ref.at[pl.ds(at, TILE), :], k_s.at[pl.ds(at, TILE), :], sem.at[0, j]
            ),
            pltpu.make_async_copy(
                values_ref.at[pl.ds(at, TILE), :], v_s.at[pl.ds(at, TILE), :], sem.at[1, j]
            ),
        )

    def begin(j, carry):
        for copy in copies(j):
            copy.start()
        return carry

    lax.fori_loop(0, tiles, begin, 0)
    for h in range(8):
        q_s[h * BLK : (h + 1) * BLK, :] = q_ref[:, h * HD : (h + 1) * HD]
    acc[...] = jnp.zeros_like(acc)
    best[...] = jnp.full_like(best, masked_score)
    total[...] = jnp.zeros_like(total)

    def score(j):
        at = pl.multiple_of(j * TILE, TILE)
        return lax.dot_general(
            k_s[pl.ds(at, TILE), :],
            q_s[...],
            (((1,), (1,)), ((), ())),
            preferred_element_type=jnp.float32,
        )

    def absorb(j, scores):
        at = pl.multiple_of(j * TILE, TILE)
        old = best[...]
        new = jnp.maximum(old, jnp.max(scores, axis=0, keepdims=True))
        weights = jnp.exp2((scores - new) * factor)
        shrink = jnp.exp2((old - new) * factor)
        total[...] = total[...] * shrink + jnp.sum(weights, axis=0, keepdims=True)
        best[...] = new
        acc[...] = acc[...] * shrink + lax.dot_general(
            v_s[pl.ds(at, TILE), :],
            weights.astype(jnp.bfloat16),
            (((0,), (0,)), ((), ())),
            preferred_element_type=jnp.float32,
        )

    copies(0)[0].wait()
    s_s[0] = score(0)

    def full_tile(j, carry):
        copies(j + 1)[0].wait()
        copies(j)[1].wait()
        scores = s_s[j % 2]
        s_s[(j + 1) % 2] = score(j + 1)
        absorb(j, scores)
        return carry

    lax.fori_loop(0, tiles - 1, full_tile, 0)
    last = tiles - 1
    copies(last)[1].wait()
    key_at = last * TILE + lax.broadcasted_iota(jnp.int32, (TILE, rows), 0)
    query_at = block * BLK + lax.broadcasted_iota(jnp.int32, (TILE, rows), 1) % BLK
    absorb(last, jnp.where(key_at <= query_at, s_s[last % 2], masked_score))
    result = acc[...] / total[...]
    for h in range(8):
        part = result[:, h * BLK : (h + 1) * BLK]
        out_ref[:, h * HD : (h + 1) * HD] = part.T.astype(jnp.bfloat16)


def attention(chunk, own, queries, keys, values):
    anywhere = pl.BlockSpec(memory_space=pl.ANY)
    total = 64 * BLK
    rows = 8 * BLK
    return pl.pallas_call(
        functools.partial(attend, chunk),
        out_shape=jax.ShapeDtypeStruct((BLK, rows), jnp.bfloat16),
        grid=(1,),
        in_specs=[
            pl.BlockSpec(memory_space=pltpu.SMEM),
            pl.BlockSpec((BLK, rows), lambda i: (chunk, 0)),
            anywhere,
            anywhere,
        ],
        out_specs=pl.BlockSpec((BLK, rows), lambda i: (0, 0)),
        scratch_shapes=[
            pltpu.VMEM((total, HD), jnp.bfloat16),
            pltpu.VMEM((total, HD), jnp.bfloat16),
            pltpu.VMEM((rows, HD), jnp.bfloat16),
            pltpu.VMEM((2, TILE, rows), jnp.float32),
            pltpu.VMEM((HD, rows), jnp.float32),
            pltpu.VMEM((1, rows), jnp.float32),
            pltpu.VMEM((1, rows), jnp.float32),
            pltpu.SemaphoreType.DMA((2, total // TILE)),
        ],
        compiler_params=pltpu.CompilerParams(vmem_limit_bytes=VMEM_BYTES),
        cost_estimate=pl.CostEstimate(
            flops=10_000_000_000, bytes_accessed=1 << 22, transcendentals=0
        ),
        name="attend",
    )(own, queries, keys, values)


def project_body(n_chunks, has_sum, *refs):
    pieces, rest = refs[: 4 * n_chunks], refs[4 * n_chunks :]
    if has_sum:
        w_ref, sum_ref, out_ref, a_s, sem = rest
    else:
        w_ref, out_ref, a_s, sem = rest

    @pl.when(pl.program_id(0) == 0)
    def _():
        copies = [
            pltpu.make_async_copy(
                pieces[i * 4 + dz],
                a_s.at[pl.ds(i * BLK, BLK), pl.ds(dz * 1024, 1024)],
                sem.at[i * 4 + dz],
            )
            for i in range(n_chunks)
            for dz in range(4)
        ]
        for copy in copies:
            copy.start()
        for copy in copies:
            copy.wait()

    result = jnp.dot(
        a_s[...], w_ref[...].reshape(4096, 256), preferred_element_type=jnp.float32
    )
    if has_sum:
        result = result + sum_ref[...].astype(jnp.float32)
    out_ref[...] = result.astype(jnp.bfloat16)


def project(pieces, weight, other=None):
    n_chunks = len(pieces)
    rows = n_chunks * BLK
    anywhere = pl.BlockSpec(memory_space=pl.ANY)
    tile = pl.BlockSpec((rows, 256), lambda n: (0, n))
    flat = [piece for chunk in pieces for piece in chunk]
    return pl.pallas_call(
        functools.partial(project_body, n_chunks, other is not None),
        out_shape=jax.ShapeDtypeStruct((rows, 1024), jnp.bfloat16),
        grid=(4,),
        in_specs=[anywhere] * len(flat)
        + [pl.BlockSpec((8, None, 512, 256), lambda n: (0, n // 2, 0, n % 2))]
        + ([tile] if other is not None else []),
        out_specs=tile,
        scratch_shapes=[
            pltpu.VMEM((rows, 4096), jnp.bfloat16),
            pltpu.SemaphoreType.DMA((4 * n_chunks,)),
        ],
        compiler_params=pltpu.CompilerParams(vmem_limit_bytes=VMEM_BYTES),
        cost_estimate=pl.CostEstimate(
            flops=2 * rows * 4096 * 1024, bytes_accessed=10 << 20, transcendentals=0
        ),
        name="project",
    )(*flat, weight.reshape(8, 2, 512, 512), *([other] if other is not None else []))


def spread_target(half):
    def target(y, xl, xh, z):
        plane = (y % 2) * 2 + xl
        other = (y // 2) ^ xh
        part = half if other else 1 - half
        return ((z - plane) % 4, part, xh, plane)

    return target


def per_device(queries, keys, values, positions, out_weight):
    y, xl, xh = lax.axis_index("y"), lax.axis_index("xl"), lax.axis_index("xh")
    own = positions[::BLK] // BLK
    ids = jnp.broadcast_to(own.astype(jnp.bfloat16)[None, :, None], (4, 4, HD)).reshape(16, HD)
    packet = jnp.concatenate([keys, values, ids])
    received = [packet] + [
        move(packet, ("y", "xl"), lambda a, b, dy=dy, dx=dx: (a + dy, b + dx))
        for dy, dx in ((1, 0), (3, 0), (0, 1), (1, 1), (3, 1), (2, 0), (2, 1))
    ]
    out_weight, received[1] = lax.optimization_barrier((out_weight, received[1]))

    other = (y // 2) ^ xh
    first = lax.dynamic_slice_in_dim(out_weight, (1 - other) * 512, 512, 0)
    second = lax.dynamic_slice_in_dim(out_weight, other * 512, 512, 0)
    plane = ("y", "xl", "xh", "z")
    got_first = move(first, plane, spread_target(0))
    got_second = move(second, plane, spread_target(1))
    for_partner = jnp.where(xl == 0, got_first, got_second)
    for_self = jnp.where(xl == 0, got_second, got_first)
    ready = lax.optimization_barrier((for_partner, for_self, *received))
    for_partner, for_self, received = ready[0], ready[1], list(ready[2:])
    weight_partner = lax.all_gather(for_partner, ("y", "xl", "c"))
    weight_self = lax.all_gather(for_self, ("y", "xl", "c"))

    received = received + [move(r, ("c",), lambda a: (a + 1,)) for r in received]
    slots = jnp.concatenate([r[1024:1028, 0] for r in received]).astype(jnp.int32)
    sorted_keys, sorted_values = sorted_kv(slots, received)

    pieces = []
    for i in range(4):
        piece = attention(i, own, queries, sorted_keys, sorted_values)
        pieces.append([piece] + [move(piece, ("z",), lambda a, dz=dz: (a - dz,)) for dz in (1, 2, 3)])
    partner_sum = project(pieces, weight_partner)
    got_sum = move(partner_sum, ("xh",), lambda a: (a + 1,))
    return project(pieces, weight_self, got_sum)


def solution(mesh):
    split = Mesh(mesh.devices.reshape([SIZES[a] for a in AXES]), AXES)
    seq, head = ("y", "xl", "c"), ("xh", "z")
    placed = (P(seq, head), P(seq, head), P(seq, head), P(seq), P(head, seq))
    return jax.shard_map(
        per_device, mesh=split, in_specs=placed, out_specs=P(seq, head), check_vma=False
    )
```

time: 439 us -> 232 us (0.53); the launches traced: 437 us -> 235 us
  matrix products: 91.9 us -> 0 us
  Pallas kernels: 0 us -> 79 us
  waiting for transfers between devices: 171 us -> 95 us
  other arithmetic: 63.7 us -> 3.32 us
  loops' own time: 19.5 us -> 0 us
  starting transfers between devices: 54.2 us -> 36.8 us
  blocking collectives: 17.2 us -> 0 us
    reduce_scatter x1 -> x0, waiting for transfers between devices: 126 us -> none  [per_device(): lax.psum_scatter(terms, 'head', scatter_dimension=1, tiled=True)]
    dot_general x33 -> x0, matrix products: 91.9 us -> none  [the longest x16 49.9 us: update(): jnp.einsum('grqk,kgd->grqd', weights.astype(jnp.bfloat16), values_split,...]
    pallas_call x0 -> x7, Pallas kernels: none -> 79 us  [the longest x4 52.1 us: attention(): pl.pallas_call(functools.partial(attend, chunk), out_shape=jax.ShapeDtype...]
    ppermute x15 -> x30, waiting for transfers between devices: 43.9 us -> 94.3 us  [move(): return lax.ppermute(block, axes, route)]
    reduce_sum x16 -> x0, other arithmetic: 32.5 us -> none  [update(): total_new = total_old * factor + jnp.sum(weights, axis=-1)]
    another operation x17 -> x0, loops' own time: 19.5 us -> none  [the longest x1 18.1 us: per_device(): lax.fori_loop(1, seq_count, cycle_step, (running, kv_pair))]
    ppermute x15 -> x30, starting transfers between devices: 54.1 us -> 36.7 us  [move(): return lax.ppermute(block, axes, route)]
    all_gather x1 -> x0, blocking collectives: 17.2 us -> none  [per_device(): all_positions = lax.all_gather(positions, 'seq', axis=0, tiled=True)]
  transfers between devices with their start and end apart: 17 -> 32, of which waited for: 16 -> 12; matrix products, arithmetic and copies ran while one was open for 33% -> 2% of each run, Pallas kernels for 0% -> 29%
where the time goes in v1:
time: 232 us; the launch traced here: 235 us
  waiting for transfers between devices  95 us (41%)
  Pallas kernels  79 us (34%)
  starting transfers between devices  36.8 us (16%)
  between operations  13.9 us (6%)
  local copies, waits for them, and re-layouts  6.81 us (3%)
  other arithmetic  3.32 us (1%)
    ppermute x30, waiting for transfers between devices, move(): return lax.ppermute(block, axes, route)  94.3 us
    pallas_call x4, Pallas kernels, attention(): pl.pallas_call(functools.partial(attend, chunk), out_shape=jax.ShapeDtype...  52.1 us
    ppermute x30, starting transfers between devices, move(): return lax.ppermute(block, axes, route)  36.7 us
    pallas_call x2, Pallas kernels, project(): pl.pallas_call(functools.partial(project_body, n_chunks, other is not Non...  21 us
    pallas_call x1, Pallas kernels, sorted_kv(): pl.pallas_call(sort_blocks, out_shape=(sorted_shape, sorted_shape), in_sp...  5.94 us
  transfers between devices with their start and end apart: 32, of which 12 were waited for; matrix products, arithmetic and copies ran while one was open for 2% of the time, Pallas kernels for 29%

profile of v1, /device:TPU:25, one launch (start us, length us, event | category | flops | bytes accessed | tf_op | source)
XLA Modules:
  0.0 234.8 jit_solution(4428363566879414385)
XLA Ops:
  6.5 0.8 slice.51
  7.3 0.5 fusion
  7.9 1.2 maximum_maximum_fusion.refs_0_
  9.2 7.2 %collective-permute-done.refs_1_ = bf16[1040,128]{1,0:T(8,128)(2,1)S(1)} collective-permute-done((bf16[1040,128]{1,0:T(8,128)(2,1)S(1)}, bf16[1040,128]{1,0:T(8,128)(2,1)S(1)}, u32[]{:S(2)}, u32[]{:S(2)}) %collective-permute-start) | collective-permute-done | bytes 266272 | tf_op jit(solution)/shard_map/ppermute | solution.py:35
  16.5 1.4 constant_dynamic-slice_fusion
  17.8 5.7 %collective-permute-start.1 = (bf16[512,512]{1,0:T(8,128)(2,1)S(1)}, bf16[512,512]{1,0:T(8,128)(2,1)S(1)}, u32[]{:S(2)}, u32[]{:S(2)}) collective-permute-start(bf16[512,512]{1,0:T(8,128)(2,1)S(1)} %get-tuple-element.38), channel_id=1, source_target_pairs={{0,16},{1,48},{2,80},{3,112},{4,4},{5,36},{6,68},{7,100},{16,113},... | collective-permute-start | bytes 1572872 | tf_op jit(solution)/shard_map/ppermute | solution.py:35
  23.5 2.8 %collective-permute-start.2 = (bf16[512,512]{1,0:T(8,128)(2,1)S(1)}, bf16[512,512]{1,0:T(8,128)(2,1)S(1)}, u32[]{:S(2)}, u32[]{:S(2)}) collective-permute-start(bf16[512,512]{1,0:T(8,128)(2,1)S(1)} %get-tuple-element.37), channel_id=1, source_target_pairs={{0,0},{1,32},{2,64},{3,96},{4,20},{5,52},{6,84},{7,116},{16,97},{1... | collective-permute-start | bytes 1572872 | tf_op jit(solution)/shard_map/ppermute | solution.py:35
  26.4 0.9 collective-permute-start.3
  27.3 1.7 collective-permute-start.4
  29.0 2.3 collective-permute-start.5
  31.3 20.3 %collective-permute-done.3.refs_2_ = bf16[1040,128]{1,0:T(8,128)(2,1)S(1)} collective-permute-done((bf16[1040,128]{1,0:T(8,128)(2,1)S(1)}, bf16[1040,128]{1,0:T(8,128)(2,1)S(1)}, u32[]{:S(2)}, u32[]{:S(2)}) %collective-permute-start.3) | collective-permute-done | bytes 266272 | tf_op jit(solution)/shard_map/ppermute | solution.py:35
  51.6 5.5 %collective-permute-start.6 = (bf16[1040,128]{1,0:T(8,128)(2,1)S(1)}, bf16[1040,128]{1,0:T(8,128)(2,1)S(1)}, u32[]{:S(2)}, u32[]{:S(2)}) collective-permute-start(bf16[1040,128]{1,0:T(8,128)(2,1)S(1)} %maximum_maximum_fusion.refs_0_), channel_id=1, source_target_pairs={{0,112},{16,96},{32,16},{48,0},{64,48},{80,32},{96,80},{112,64},{1... | collective-permute-start | bytes 798728 | tf_op jit(solution)/shard_map/ppermute | solution.py:35
  57.1 0.8 collective-permute-start.8
  58.0 1.0 broadcast_select_fusion
  59.0 1.8 collective-permute-done.6.refs_5_
  60.8 16.0 %collective-permute-done.7.refs_6_ = bf16[1040,128]{1,0:T(8,128)(2,1)S(1)} collective-permute-done((bf16[1040,128]{1,0:T(8,128)(2,1)S(1)}, bf16[1040,128]{1,0:T(8,128)(2,1)S(1)}, u32[]{:S(2)}, u32[]{:S(2)}) %collective-permute-start.7) | collective-permute-done | bytes 266272 | tf_op jit(solution)/shard_map/ppermute | solution.py:35
  76.9 0.7 all-gather.5.cloned.1.call-update
  77.6 2.1 collective-permute-start.16
  79.8 0.4 collective-permute-start.14
  80.3 0.1 slice_reduce_fusion.8
  80.4 0.8 slice_reduce_fusion.10
  81.2 0.5 collective-permute-start.12
  81.7 0.1 slice_reduce_fusion.12
  81.8 0.1 slice_reduce_fusion.14
  82.0 0.2 collective-permute-start.11
  82.1 0.1 slice_reduce_fusion
  82.3 0.5 collective-permute-start.10
  82.8 0.1 slice_reduce_fusion.1
  82.9 0.2 collective-permute-start.9
  83.1 0.1 slice_reduce_fusion.2
  83.2 0.1 slice_reduce_fusion.3
  83.3 0.1 slice_reduce_fusion.4
  83.4 0.1 collective-permute-done.11.refs_10_
  83.6 0.1 slice_reduce_fusion.5
  83.7 0.3 collective-permute-done.10.refs_9_
  84.0 0.1 slice_reduce_fusion.6
  84.1 0.4 collective-permute-done.9.refs_8_
  84.5 0.1 slice_reduce_fusion.7
  84.7 0.6 copy-done.15
  85.2 0.1 concatenate.7
  85.3 0.6 convert_element_type.7.slot_ref
  86.0 5.9 %sort_blocks.1 = (bf16[8192,128]{1,0:T(8,128)(2,1)}, bf16[8192,128]{1,0:T(8,128)(2,1)}) custom-call(s32[64]{0:T(128)} %convert_element_type.7.slot_ref, bf16[1040,128]{1,0:T(8,128)(2,1)} %copy-done, bf16[1040,128]{1,0:T(8,128)(2,1)} %copy-done.1, bf16[1040,128]{1,0:T(8,128)(2,1)} %copy-done.2, bf16[1040,128]{1,0:T(8,128)(2,1)} %copy-done.3, ...), custom_call_target="tpu_custom_call" | custom-call | bytes 8388608 | tf_op jit(solution)/shard_map/sort_blocks/pallas_call | solution.py:62
  91.9 11.8 %attend.7.refs_12_ = bf16[128,1024]{1,0:T(8,128)(2,1)} custom-call(s32[4]{0:T(128)} %get-tuple-element.34.own_ref, bf16[512,1024]{1,0:T(8,128)(2,1)} %q_ref.7, bf16[8192,128]{1,0:T(8,128)(2,1)} %get-tuple-element.29.keys_ref, bf16[8192,128]{1,0:T(8,128)(2,1)} %get-tuple-element.30.values_ref), custom_call_target="tpu_custom_call" | custom-call | flops 10000000000 | bytes 4194304 | tf_op jit(solution)/shard_map/attend/pallas_call | solution.py:153
  103.9 1.4 collective-permute-start.28
  105.3 10.9 %attend.6.refs_8_ = bf16[128,1024]{1,0:T(8,128)(2,1)} custom-call(s32[4]{0:T(128)} %get-tuple-element.34.own_ref, bf16[512,1024]{1,0:T(8,128)(2,1)} %q_ref.7, bf16[8192,128]{1,0:T(8,128)(2,1)} %get-tuple-element.29.keys_ref, bf16[8192,128]{1,0:T(8,128)(2,1)} %get-tuple-element.30.values_ref), custom_call_target="tpu_custom_call" | custom-call | flops 10000000000 | bytes 4194304 | tf_op jit(solution)/shard_map/attend/pallas_call | solution.py:153
  116.2 2.6 %collective-permute-start.23 = (bf16[128,1024]{1,0:T(8,128)(2,1)}, bf16[128,1024]{1,0:T(8,128)(2,1)S(1)}, u32[]{:S(2)}, u32[]{:S(2)}) collective-permute-start(bf16[128,1024]{1,0:T(8,128)(2,1)} %attend.6.refs_8_), channel_id=1, source_target_pairs={{0,3},{1,0},{2,1},{3,2},{4,7},{5,4},{6,5},{7,6},{8,11},{9,8},{10,9... | collective-permute-start | bytes 786440 | tf_op jit(solution)/shard_map/ppermute | solution.py:35
  118.8 1.3 collective-permute-start.24
  120.1 14.3 %attend.5.refs_4_ = bf16[128,1024]{1,0:T(8,128)(2,1)} custom-call(s32[4]{0:T(128)} %get-tuple-element.34.own_ref, bf16[512,1024]{1,0:T(8,128)(2,1)} %q_ref.7, bf16[8192,128]{1,0:T(8,128)(2,1)} %get-tuple-element.29.keys_ref, bf16[8192,128]{1,0:T(8,128)(2,1)} %get-tuple-element.30.values_ref), custom_call_target="tpu_custom_call" | custom-call | flops 10000000000 | bytes 4194304 | tf_op jit(solution)/shard_map/attend/pallas_call | solution.py:153
  134.5 0.8 collective-permute-start.25
  135.3 1.9 collective-permute-start.20
  137.2 15.1 %attend.4.refs_0_ = bf16[128,1024]{1,0:T(8,128)(2,1)} custom-call(s32[4]{0:T(128)} %get-tuple-element.34.own_ref, bf16[512,1024]{1,0:T(8,128)(2,1)} %q_ref.7, bf16[8192,128]{1,0:T(8,128)(2,1)} %get-tuple-element.29.keys_ref, bf16[8192,128]{1,0:T(8,128)(2,1)} %get-tuple-element.30.values_ref), custom_call_target="tpu_custom_call" | custom-call | flops 10000000000 | bytes 4194304 | tf_op jit(solution)/shard_map/attend/pallas_call | solution.py:153
  152.4 0.5 collective-permute-start.21
  152.9 0.2 collective-permute-start.22
  153.2 2.5 %collective-permute-start.17 = (bf16[128,1024]{1,0:T(8,128)(2,1)}, bf16[128,1024]{1,0:T(8,128)(2,1)S(1)}, u32[]{:S(2)}, u32[]{:S(2)}) collective-permute-start(bf16[128,1024]{1,0:T(8,128)(2,1)} %attend.4.refs_0_), channel_id=1, source_target_pairs={{0,3},{1,0},{2,1},{3,2},{4,7},{5,4},{6,5},{7,6},{8,11},{9,8},{10,9... | collective-permute-start | bytes 786440 | tf_op jit(solution)/shard_map/ppermute | solution.py:35
  155.6 1.3 collective-permute-start.18
  156.9 4.9 %collective-permute-done.21.refs_6_ = bf16[128,1024]{1,0:T(8,128)(2,1)S(1)} collective-permute-done((bf16[128,1024]{1,0:T(8,128)(2,1)S(1)}, bf16[128,1024]{1,0:T(8,128)(2,1)S(1)}, u32[]{:S(2)}, u32[]{:S(2)}) %collective-permute-start.21) | collective-permute-done | bytes 262176 | tf_op jit(solution)/shard_map/ppermute | solution.py:35
  161.8 6.4 %collective-permute-done.22.refs_7_ = bf16[128,1024]{1,0:T(8,128)(2,1)S(1)} collective-permute-done((bf16[128,1024]{1,0:T(8,128)(2,1)S(1)}, bf16[128,1024]{1,0:T(8,128)(2,1)S(1)}, u32[]{:S(2)}, u32[]{:S(2)}) %collective-permute-start.22) | collective-permute-done | bytes 262176 | tf_op jit(solution)/shard_map/ppermute | solution.py:35
  168.3 4.8 %collective-permute-done.18.refs_2_ = bf16[128,1024]{1,0:T(8,128)(2,1)S(1)} collective-permute-done((bf16[128,1024]{1,0:T(8,128)(2,1)}, bf16[128,1024]{1,0:T(8,128)(2,1)S(1)}, u32[]{:S(2)}, u32[]{:S(2)}) %collective-permute-start.18) | collective-permute-done | bytes 262176 | tf_op jit(solution)/shard_map/ppermute | solution.py:35
  173.1 6.0 %collective-permute-done.19.refs_3_ = bf16[128,1024]{1,0:T(8,128)(2,1)S(1)} collective-permute-done((bf16[128,1024]{1,0:T(8,128)(2,1)}, bf16[128,1024]{1,0:T(8,128)(2,1)S(1)}, u32[]{:S(2)}, u32[]{:S(2)}) %collective-permute-start.19) | collective-permute-done | bytes 262176 | tf_op jit(solution)/shard_map/ppermute | solution.py:35
  179.2 0.6 copy-done.30
  179.8 10.5 %project.2 = bf16[512,1024]{1,0:T(8,128)(2,1)} custom-call(bf16[128,1024]{1,0:T(8,128)(2,1)} %attend.4.refs_0_, bf16[128,1024]{1,0:T(8,128)(2,1)} %copy-done.28, bf16[128,1024]{1,0:T(8,128)(2,1)} %copy-done.29, bf16[128,1024]{1,0:T(8,128)(2,1)} %copy-done.30, bf16[128,1024]{1,0:T(8,128)(2,1)} %attend.5.refs_4_, bf16[128,1024]{1,0:T(8,128)(2,1)} %copy-done.25, ...), custom_call_target="tpu_custom_call" | custom-call | flops 4294967296 | bytes 10485760 | tf_op jit(solution)/shard_map/project/pallas_call | solution.py:219
  190.4 26.0 %collective-permute-done.29.refs_17_ = bf16[512,1024]{1,0:T(8,128)(2,1)S(1)} collective-permute-done((bf16[512,1024]{1,0:T(8,128)(2,1)}, bf16[512,1024]{1,0:T(8,128)(2,1)S(1)}, u32[]{:S(2)}, u32[]{:S(2)}) %collective-permute-start.29) | collective-permute-done | bytes 1048608 | tf_op jit(solution)/shard_map/ppermute | solution.py:35
  216.4 1.1 copy-done.16
  217.5 10.5 %project.3 = bf16[512,1024]{1,0:T(8,128)(2,1)} custom-call(bf16[128,1024]{1,0:T(8,128)(2,1)} %attend.4.refs_0_, bf16[128,1024]{1,0:T(8,128)(2,1)} %copy-done.28, bf16[128,1024]{1,0:T(8,128)(2,1)} %copy-done.29, bf16[128,1024]{1,0:T(8,128)(2,1)} %copy-done.30, bf16[128,1024]{1,0:T(8,128)(2,1)} %attend.5.refs_4_, bf16[128,1024]{1,0:T(8,128)(2,1)} %copy-done.25, ...), custom_call_target="tpu_custom_call" | custom-call | flops 4294967296 | bytes 10485760 | tf_op jit(solution)/shard_map/project/pallas_call | solution.py:219
  (93 shorter events, 0.9 us)
Async XLA Ops:
  6.5 172.5 %all-gather.7.cloned.1.call-start = ((), (), s32[]{:S(2)}) async-start(), calls=%async_computation.1 | async-start | bytes 8912896 | tf_op jit(solution)/shard_map/all_gather | solution.py:270
  9.1 76.8 %copy-start = (bf16[1040,128]{1,0:T(8,128)(2,1)}, bf16[1040,128]{1,0:T(8,128)(2,1)S(1)}, u32[]{:S(2)}) copy-start(bf16[1040,128]{1,0:T(8,128)(2,1)S(1)} %maximum_maximum_fusion.refs_0_) | copy-start | bytes 798724
  9.1 7.3 %collective-permute-start = (bf16[1040,128]{1,0:T(8,128)(2,1)S(1)}, bf16[1040,128]{1,0:T(8,128)(2,1)S(1)}, u32[]{:S(2)}, u32[]{:S(2)}) collective-permute-start(bf16[1040,128]{1,0:T(8,128)(2,1)S(1)} %maximum_maximum_fusion.refs_0_), channel_id=1, source_target_pairs={{0,32},{16,48},{32,64},{48,80},{64,96},{80,112},{96,0},{112,16},{1... | collective-permute-start | bytes 798728 | tf_op jit(solution)/shard_map/ppermute | solution.py:35
  16.5 69.5 %copy-start.1 = (bf16[1040,128]{1,0:T(8,128)(2,1)}, bf16[1040,128]{1,0:T(8,128)(2,1)S(1)}, u32[]{:S(2)}) copy-start(bf16[1040,128]{1,0:T(8,128)(2,1)S(1)} %collective-permute-done.refs_1_) | copy-start | bytes 798724
  17.8 39.3 %collective-permute-start.1 = (bf16[512,512]{1,0:T(8,128)(2,1)S(1)}, bf16[512,512]{1,0:T(8,128)(2,1)S(1)}, u32[]{:S(2)}, u32[]{:S(2)}) collective-permute-start(bf16[512,512]{1,0:T(8,128)(2,1)S(1)} %get-tuple-element.38), channel_id=1, source_target_pairs={{0,16},{1,48},{2,80},{3,112},{4,4},{5,36},{6,68},{7,100},{16,113},... | collective-permute-start | bytes 1572872 | tf_op jit(solution)/shard_map/ppermute | solution.py:35
  23.5 33.6 %collective-permute-start.2 = (bf16[512,512]{1,0:T(8,128)(2,1)S(1)}, bf16[512,512]{1,0:T(8,128)(2,1)S(1)}, u32[]{:S(2)}, u32[]{:S(2)}) collective-permute-start(bf16[512,512]{1,0:T(8,128)(2,1)S(1)} %get-tuple-element.37), channel_id=1, source_target_pairs={{0,0},{1,32},{2,64},{3,96},{4,20},{5,52},{6,84},{7,116},{16,97},{1... | collective-permute-start | bytes 1572872 | tf_op jit(solution)/shard_map/ppermute | solution.py:35
  26.4 25.2 %collective-permute-start.3 = (bf16[1040,128]{1,0:T(8,128)(2,1)S(1)}, bf16[1040,128]{1,0:T(8,128)(2,1)S(1)}, u32[]{:S(2)}, u32[]{:S(2)}) collective-permute-start(bf16[1040,128]{1,0:T(8,128)(2,1)S(1)} %maximum_maximum_fusion.refs_0_), channel_id=1, source_target_pairs={{0,96},{16,112},{32,0},{48,16},{64,32},{80,48},{96,64},{112,80},{1... | collective-permute-start | bytes 798728 | tf_op jit(solution)/shard_map/ppermute | solution.py:35
  27.3 31.7 %collective-permute-start.4 = (bf16[1040,128]{1,0:T(8,128)(2,1)S(1)}, bf16[1040,128]{1,0:T(8,128)(2,1)S(1)}, u32[]{:S(2)}, u32[]{:S(2)}) collective-permute-start(bf16[1040,128]{1,0:T(8,128)(2,1)S(1)} %maximum_maximum_fusion.refs_0_), channel_id=1, source_target_pairs={{0,16},{16,0},{32,48},{48,32},{64,80},{80,64},{96,112},{112,96},{1... | collective-permute-start | bytes 798728 | tf_op jit(solution)/shard_map/ppermute | solution.py:35
  29.0 30.0 %collective-permute-start.5 = (bf16[1040,128]{1,0:T(8,128)(2,1)S(1)}, bf16[1040,128]{1,0:T(8,128)(2,1)S(1)}, u32[]{:S(2)}, u32[]{:S(2)}) collective-permute-start(bf16[1040,128]{1,0:T(8,128)(2,1)S(1)} %maximum_maximum_fusion.refs_0_), channel_id=1, source_target_pairs={{0,48},{16,32},{32,80},{48,64},{64,112},{80,96},{96,16},{112,0},{1... | collective-permute-start | bytes 798728 | tf_op jit(solution)/shard_map/ppermute | solution.py:35
  51.6 34.3 %copy-start.2 = (bf16[1040,128]{1,0:T(8,128)(2,1)}, bf16[1040,128]{1,0:T(8,128)(2,1)S(1)}, u32[]{:S(2)}) copy-start(bf16[1040,128]{1,0:T(8,128)(2,1)S(1)} %collective-permute-done.3.refs_2_) | copy-start | bytes 798724
  51.6 9.2 %collective-permute-start.6 = (bf16[1040,128]{1,0:T(8,128)(2,1)S(1)}, bf16[1040,128]{1,0:T(8,128)(2,1)S(1)}, u32[]{:S(2)}, u32[]{:S(2)}) collective-permute-start(bf16[1040,128]{1,0:T(8,128)(2,1)S(1)} %maximum_maximum_fusion.refs_0_), channel_id=1, source_target_pairs={{0,112},{16,96},{32,16},{48,0},{64,48},{80,32},{96,80},{112,64},{1... | collective-permute-start | bytes 798728 | tf_op jit(solution)/shard_map/ppermute | solution.py:35
  57.1 19.7 %collective-permute-start.7 = (bf16[1040,128]{1,0:T(8,128)(2,1)S(1)}, bf16[1040,128]{1,0:T(8,128)(2,1)S(1)}, u32[]{:S(2)}, u32[]{:S(2)}) collective-permute-start(bf16[1040,128]{1,0:T(8,128)(2,1)S(1)} %maximum_maximum_fusion.refs_0_), channel_id=1, source_target_pairs={{0,64},{16,80},{32,96},{48,112},{64,0},{80,16},{96,32},{112,48},{1... | collective-permute-start | bytes 798728 | tf_op jit(solution)/shard_map/ppermute | solution.py:35
  57.1 19.7 %collective-permute-start.8 = (bf16[1040,128]{1,0:T(8,128)(2,1)S(1)}, bf16[1040,128]{1,0:T(8,128)(2,1)S(1)}, u32[]{:S(2)}, u32[]{:S(2)}) collective-permute-start(bf16[1040,128]{1,0:T(8,128)(2,1)S(1)} %maximum_maximum_fusion.refs_0_), channel_id=1, source_target_pairs={{0,80},{16,64},{32,112},{48,96},{64,16},{80,0},{96,48},{112,32},{1... | collective-permute-start | bytes 798728 | tf_op jit(solution)/shard_map/ppermute | solution.py:35
  59.0 26.9 %copy-start.3 = (bf16[1040,128]{1,0:T(8,128)(2,1)}, bf16[1040,128]{1,0:T(8,128)(2,1)S(1)}, u32[]{:S(2)}) copy-start(bf16[1040,128]{1,0:T(8,128)(2,1)S(1)} %collective-permute-done.4.refs_3_) | copy-start | bytes 798724
  59.0 26.9 %copy-start.4 = (bf16[1040,128]{1,0:T(8,128)(2,1)}, bf16[1040,128]{1,0:T(8,128)(2,1)S(1)}, u32[]{:S(2)}) copy-start(bf16[1040,128]{1,0:T(8,128)(2,1)S(1)} %collective-permute-done.5.refs_4_) | copy-start | bytes 798724
  60.8 16.0 %copy-start.5 = (bf16[1040,128]{1,0:T(8,128)(2,1)}, bf16[1040,128]{1,0:T(8,128)(2,1)S(1)}, u32[]{:S(2)}) copy-start(bf16[1040,128]{1,0:T(8,128)(2,1)S(1)} %collective-permute-done.6.refs_5_) | copy-start | bytes 798724
  76.8 9.2 %copy-start.6 = (bf16[1040,128]{1,0:T(8,128)(2,1)}, bf16[1040,128]{1,0:T(8,128)(2,1)S(1)}, u32[]{:S(2)}) copy-start(bf16[1040,128]{1,0:T(8,128)(2,1)S(1)} %collective-permute-done.7.refs_6_) | copy-start | bytes 798724
  76.8 9.2 %copy-start.7 = (bf16[1040,128]{1,0:T(8,128)(2,1)}, bf16[1040,128]{1,0:T(8,128)(2,1)S(1)}, u32[]{:S(2)}) copy-start(bf16[1040,128]{1,0:T(8,128)(2,1)S(1)} %collective-permute-done.8.refs_7_) | copy-start | bytes 798724
  76.8 113.6 %all-gather.5.cloned.1.call-start = ((), (), s32[]{:S(2)}) async-start(), calls=%async_computation | async-start | bytes 8912896 | tf_op jit(solution)/shard_map/all_gather | solution.py:271
  77.6 4.4 %collective-permute-start.16 = (bf16[1040,128]{1,0:T(8,128)(2,1)S(1)}, bf16[1040,128]{1,0:T(8,128)(2,1)S(1)}, u32[]{:S(2)}, u32[]{:S(2)}) collective-permute-start(bf16[1040,128]{1,0:T(8,128)(2,1)S(1)} %collective-permute-done.8.refs_7_), channel_id=1, source_target_pairs={{0,8},{8,0},{1,9},{9,1},{2,10},{10,2},{3,11},{11,3},{4,12},{12,4},... | collective-permute-start | bytes 798728 | tf_op jit(solution)/shard_map/ppermute | solution.py:35
  79.7 2.6 %collective-permute-start.15 = (bf16[1040,128]{1,0:T(8,128)(2,1)S(1)}, bf16[1040,128]{1,0:T(8,128)(2,1)S(1)}, u32[]{:S(2)}, u32[]{:S(2)}) collective-permute-start(bf16[1040,128]{1,0:T(8,128)(2,1)S(1)} %collective-permute-done.7.refs_6_), channel_id=1, source_target_pairs={{0,8},{8,0},{1,9},{9,1},{2,10},{10,2},{3,11},{11,3},{4,12},{12,4},... | collective-permute-start | bytes 798728 | tf_op jit(solution)/shard_map/ppermute | solution.py:35
  79.8 3.1 %collective-permute-start.14 = (bf16[1040,128]{1,0:T(8,128)(2,1)}, bf16[1040,128]{1,0:T(8,128)(2,1)S(1)}, u32[]{:S(2)}, u32[]{:S(2)}) collective-permute-start(bf16[1040,128]{1,0:T(8,128)(2,1)} %copy-done.5), channel_id=1, source_target_pairs={{0,8},{8,0},{1,9},{9,1},{2,10},{10,2},{3,11},{11,3},{4,12},{12,4},... | collective-permute-start | bytes 798728 | tf_op jit(solution)/shard_map/ppermute | solution.py:35
  80.2 3.0 %collective-permute-start.13 = (bf16[1040,128]{1,0:T(8,128)(2,1)S(1)}, bf16[1040,128]{1,0:T(8,128)(2,1)S(1)}, u32[]{:S(2)}, u32[]{:S(2)}) collective-permute-start(bf16[1040,128]{1,0:T(8,128)(2,1)S(1)} %collective-permute-done.5.refs_4_), channel_id=1, source_target_pairs={{0,8},{8,0},{1,9},{9,1},{2,10},{10,2},{3,11},{11,3},{4,12},{12,4},... | collective-permute-start | bytes 798728 | tf_op jit(solution)/shard_map/ppermute | solution.py:35
  81.2 2.1 collective-permute-start.12
  82.0 4.0 %copy-start.8 = (bf16[1040,128]{1,0:T(8,128)(2,1)}, bf16[1040,128]{1,0:T(8,128)(2,1)S(1)}, u32[]{:S(2)}) copy-start(bf16[1040,128]{1,0:T(8,128)(2,1)S(1)} %collective-permute-done.16.refs_15_) | copy-start | bytes 798724
  82.0 1.6 collective-permute-start.11
  82.3 3.7 %copy-start.9 = (bf16[1040,128]{1,0:T(8,128)(2,1)}, bf16[1040,128]{1,0:T(8,128)(2,1)S(1)}, u32[]{:S(2)}) copy-start(bf16[1040,128]{1,0:T(8,128)(2,1)S(1)} %collective-permute-done.15.refs_14_) | copy-start | bytes 798724
  82.3 1.7 collective-permute-start.10
  82.9 3.1 %copy-start.10 = (bf16[1040,128]{1,0:T(8,128)(2,1)}, bf16[1040,128]{1,0:T(8,128)(2,1)S(1)}, u32[]{:S(2)}) copy-start(bf16[1040,128]{1,0:T(8,128)(2,1)S(1)} %collective-permute-done.14.refs_13_) | copy-start | bytes 798724
  82.9 1.6 collective-permute-start.9
  83.2 2.8 %copy-start.11 = (bf16[1040,128]{1,0:T(8,128)(2,1)}, bf16[1040,128]{1,0:T(8,128)(2,1)S(1)}, u32[]{:S(2)}) copy-start(bf16[1040,128]{1,0:T(8,128)(2,1)S(1)} %collective-permute-done.13.refs_12_) | copy-start | bytes 798724
  83.3 1.2 copy-start.12
  83.6 1.1 copy-start.13
  84.0 0.7 copy-start.14
  84.5 0.7 copy-start.15
  103.7 30.7 %collective-permute-start.26 = (bf16[128,1024]{1,0:T(8,128)(2,1)}, bf16[128,1024]{1,0:T(8,128)(2,1)S(1)}, u32[]{:S(2)}, u32[]{:S(2)}) collective-permute-start(bf16[128,1024]{1,0:T(8,128)(2,1)} %attend.7.refs_12_), channel_id=1, source_target_pairs={{0,3},{1,0},{2,1},{3,2},{4,7},{5,4},{6,5},{7,6},{8,11},{9,8},{10,9... | collective-permute-start | bytes 786440 | tf_op jit(solution)/shard_map/ppermute | solution.py:35
  103.8 31.5 %collective-permute-start.27 = (bf16[128,1024]{1,0:T(8,128)(2,1)}, bf16[128,1024]{1,0:T(8,128)(2,1)S(1)}, u32[]{:S(2)}, u32[]{:S(2)}) collective-permute-start(bf16[128,1024]{1,0:T(8,128)(2,1)} %attend.7.refs_12_), channel_id=1, source_target_pairs={{0,2},{1,3},{2,0},{3,1},{4,6},{5,7},{6,4},{7,5},{8,10},{9,11},{10,... | collective-permute-start | bytes 786440 | tf_op jit(solution)/shard_map/ppermute | solution.py:35
  103.9 48.5 %collective-permute-start.28 = (bf16[128,1024]{1,0:T(8,128)(2,1)}, bf16[128,1024]{1,0:T(8,128)(2,1)S(1)}, u32[]{:S(2)}, u32[]{:S(2)}) collective-permute-start(bf16[128,1024]{1,0:T(8,128)(2,1)} %attend.7.refs_12_), channel_id=1, source_target_pairs={{0,1},{1,2},{2,3},{3,0},{4,5},{5,6},{6,7},{7,4},{8,9},{9,10},{10,1... | collective-permute-start | bytes 786440 | tf_op jit(solution)/shard_map/ppermute | solution.py:35
  116.2 18.3 %copy-start.20 = (bf16[128,1024]{1,0:T(8,128)(2,1)S(1)}, bf16[128,1024]{1,0:T(8,128)(2,1)}, u32[]{:S(2)}) copy-start(bf16[128,1024]{1,0:T(8,128)(2,1)} %attend.6.refs_8_) | copy-start | bytes 786436
  116.2 36.8 %collective-permute-start.23 = (bf16[128,1024]{1,0:T(8,128)(2,1)}, bf16[128,1024]{1,0:T(8,128)(2,1)S(1)}, u32[]{:S(2)}, u32[]{:S(2)}) collective-permute-start(bf16[128,1024]{1,0:T(8,128)(2,1)} %attend.6.refs_8_), channel_id=1, source_target_pairs={{0,3},{1,0},{2,1},{3,2},{4,7},{5,4},{6,5},{7,6},{8,11},{9,8},{10,9... | collective-permute-start | bytes 786440 | tf_op jit(solution)/shard_map/ppermute | solution.py:35
  118.8 34.3 %collective-permute-start.24 = (bf16[128,1024]{1,0:T(8,128)(2,1)}, bf16[128,1024]{1,0:T(8,128)(2,1)S(1)}, u32[]{:S(2)}, u32[]{:S(2)}) collective-permute-start(bf16[128,1024]{1,0:T(8,128)(2,1)} %attend.6.refs_8_), channel_id=1, source_target_pairs={{0,2},{1,3},{2,0},{3,1},{4,6},{5,7},{6,4},{7,5},{8,10},{9,11},{10,... | collective-permute-start | bytes 786440 | tf_op jit(solution)/shard_map/ppermute | solution.py:35
  134.4 17.9 %copy-start.23 = (bf16[128,1024]{1,0:T(8,128)(2,1)S(1)}, bf16[128,1024]{1,0:T(8,128)(2,1)}, u32[]{:S(2)}) copy-start(bf16[128,1024]{1,0:T(8,128)(2,1)} %attend.5.refs_4_) | copy-start | bytes 786436
  134.5 17.9 %copy-start.17 = (bf16[128,1024]{1,0:T(8,128)(2,1)}, bf16[128,1024]{1,0:T(8,128)(2,1)S(1)}, u32[]{:S(2)}) copy-start(bf16[128,1024]{1,0:T(8,128)(2,1)S(1)} %collective-permute-done.26.refs_13_) | copy-start | bytes 786436
  134.5 21.2 %collective-permute-start.25 = (bf16[128,1024]{1,0:T(8,128)(2,1)S(1)}, bf16[128,1024]{1,0:T(8,128)(2,1)S(1)}, u32[]{:S(2)}, u32[]{:S(2)}) collective-permute-start(bf16[128,1024]{1,0:T(8,128)(2,1)S(1)} %copy-done.20), channel_id=1, source_target_pairs={{0,1},{1,2},{2,3},{3,0},{4,5},{5,6},{6,7},{7,4},{8,9},{9,10},{10,1... | collective-permute-start | bytes 786440 | tf_op jit(solution)/shard_map/ppermute | solution.py:35
  135.3 17.1 %copy-start.18 = (bf16[128,1024]{1,0:T(8,128)(2,1)}, bf16[128,1024]{1,0:T(8,128)(2,1)S(1)}, u32[]{:S(2)}) copy-start(bf16[128,1024]{1,0:T(8,128)(2,1)S(1)} %collective-permute-done.27.refs_14_) | copy-start | bytes 786436
  135.3 21.6 %collective-permute-start.20 = (bf16[128,1024]{1,0:T(8,128)(2,1)}, bf16[128,1024]{1,0:T(8,128)(2,1)S(1)}, u32[]{:S(2)}, u32[]{:S(2)}) collective-permute-start(bf16[128,1024]{1,0:T(8,128)(2,1)} %attend.5.refs_4_), channel_id=1, source_target_pairs={{0,3},{1,0},{2,1},{3,2},{4,7},{5,4},{6,5},{7,6},{8,11},{9,8},{10,9... | collective-permute-start | bytes 786440 | tf_op jit(solution)/shard_map/ppermute | solution.py:35
  152.4 26.7 %copy-start.19 = (bf16[128,1024]{1,0:T(8,128)(2,1)}, bf16[128,1024]{1,0:T(8,128)(2,1)S(1)}, u32[]{:S(2)}) copy-start(bf16[128,1024]{1,0:T(8,128)(2,1)S(1)} %collective-permute-done.28.refs_15_) | copy-start | bytes 786436
  152.4 9.4 %collective-permute-start.21 = (bf16[128,1024]{1,0:T(8,128)(2,1)S(1)}, bf16[128,1024]{1,0:T(8,128)(2,1)S(1)}, u32[]{:S(2)}, u32[]{:S(2)}) collective-permute-start(bf16[128,1024]{1,0:T(8,128)(2,1)S(1)} %copy-done.23), channel_id=1, source_target_pairs={{0,2},{1,3},{2,0},{3,1},{4,6},{5,7},{6,4},{7,5},{8,10},{9,11},{10,... | collective-permute-start | bytes 786440 | tf_op jit(solution)/shard_map/ppermute | solution.py:35
  152.9 26.1 %copy-start.21 = (bf16[128,1024]{1,0:T(8,128)(2,1)}, bf16[128,1024]{1,0:T(8,128)(2,1)S(1)}, u32[]{:S(2)}) copy-start(bf16[128,1024]{1,0:T(8,128)(2,1)S(1)} %collective-permute-done.23.refs_9_) | copy-start | bytes 786436
  152.9 15.3 %collective-permute-start.22 = (bf16[128,1024]{1,0:T(8,128)(2,1)S(1)}, bf16[128,1024]{1,0:T(8,128)(2,1)S(1)}, u32[]{:S(2)}, u32[]{:S(2)}) collective-permute-start(bf16[128,1024]{1,0:T(8,128)(2,1)S(1)} %copy-done.23), channel_id=1, source_target_pairs={{0,1},{1,2},{2,3},{3,0},{4,5},{5,6},{6,7},{7,4},{8,9},{9,10},{10,1... | collective-permute-start | bytes 786440 | tf_op jit(solution)/shard_map/ppermute | solution.py:35
  153.2 25.9 %copy-start.22 = (bf16[128,1024]{1,0:T(8,128)(2,1)}, bf16[128,1024]{1,0:T(8,128)(2,1)S(1)}, u32[]{:S(2)}) copy-start(bf16[128,1024]{1,0:T(8,128)(2,1)S(1)} %collective-permute-done.24.refs_10_) | copy-start | bytes 786436
  153.2 15.1 %collective-permute-start.17 = (bf16[128,1024]{1,0:T(8,128)(2,1)}, bf16[128,1024]{1,0:T(8,128)(2,1)S(1)}, u32[]{:S(2)}, u32[]{:S(2)}) collective-permute-start(bf16[128,1024]{1,0:T(8,128)(2,1)} %attend.4.refs_0_), channel_id=1, source_target_pairs={{0,3},{1,0},{2,1},{3,2},{4,7},{5,4},{6,5},{7,6},{8,11},{9,8},{10,9... | collective-permute-start | bytes 786440 | tf_op jit(solution)/shard_map/ppermute | solution.py:35
  155.6 23.5 %copy-start.24 = (bf16[128,1024]{1,0:T(8,128)(2,1)}, bf16[128,1024]{1,0:T(8,128)(2,1)S(1)}, u32[]{:S(2)}) copy-start(bf16[128,1024]{1,0:T(8,128)(2,1)S(1)} %collective-permute-done.25.refs_11_) | copy-start | bytes 786436
  155.6 17.4 %collective-permute-start.18 = (bf16[128,1024]{1,0:T(8,128)(2,1)}, bf16[128,1024]{1,0:T(8,128)(2,1)S(1)}, u32[]{:S(2)}, u32[]{:S(2)}) collective-permute-start(bf16[128,1024]{1,0:T(8,128)(2,1)} %attend.4.refs_0_), channel_id=1, source_target_pairs={{0,2},{1,3},{2,0},{3,1},{4,6},{5,7},{6,4},{7,5},{8,10},{9,11},{10,... | collective-permute-start | bytes 786440 | tf_op jit(solution)/shard_map/ppermute | solution.py:35
  156.9 22.2 %copy-start.25 = (bf16[128,1024]{1,0:T(8,128)(2,1)}, bf16[128,1024]{1,0:T(8,128)(2,1)S(1)}, u32[]{:S(2)}) copy-start(bf16[128,1024]{1,0:T(8,128)(2,1)S(1)} %collective-permute-done.20.refs_5_) | copy-start | bytes 786436
  156.9 22.1 %collective-permute-start.19 = (bf16[128,1024]{1,0:T(8,128)(2,1)}, bf16[128,1024]{1,0:T(8,128)(2,1)S(1)}, u32[]{:S(2)}, u32[]{:S(2)}) collective-permute-start(bf16[128,1024]{1,0:T(8,128)(2,1)} %attend.4.refs_0_), channel_id=1, source_target_pairs={{0,1},{1,2},{2,3},{3,0},{4,5},{5,6},{6,7},{7,4},{8,9},{9,10},{10,1... | collective-permute-start | bytes 786440 | tf_op jit(solution)/shard_map/ppermute | solution.py:35
  161.8 17.3 %copy-start.26 = (bf16[128,1024]{1,0:T(8,128)(2,1)}, bf16[128,1024]{1,0:T(8,128)(2,1)S(1)}, u32[]{:S(2)}) copy-start(bf16[128,1024]{1,0:T(8,128)(2,1)S(1)} %collective-permute-done.21.refs_6_) | copy-start | bytes 786436
  168.2 10.9 %copy-start.27 = (bf16[128,1024]{1,0:T(8,128)(2,1)}, bf16[128,1024]{1,0:T(8,128)(2,1)S(1)}, u32[]{:S(2)}) copy-start(bf16[128,1024]{1,0:T(8,128)(2,1)S(1)} %collective-permute-done.22.refs_7_) | copy-start | bytes 786436
  168.2 10.9 %copy-start.28 = (bf16[128,1024]{1,0:T(8,128)(2,1)}, bf16[128,1024]{1,0:T(8,128)(2,1)S(1)}, u32[]{:S(2)}) copy-start(bf16[128,1024]{1,0:T(8,128)(2,1)S(1)} %collective-permute-done.17.refs_1_) | copy-start | bytes 786436
  173.1 6.1 %copy-start.29 = (bf16[128,1024]{1,0:T(8,128)(2,1)}, bf16[128,1024]{1,0:T(8,128)(2,1)S(1)}, u32[]{:S(2)}) copy-start(bf16[128,1024]{1,0:T(8,128)(2,1)S(1)} %collective-permute-done.18.refs_2_) | copy-start | bytes 786436
  179.1 0.7 copy-start.30
  190.3 26.1 %collective-permute-start.29 = (bf16[512,1024]{1,0:T(8,128)(2,1)}, bf16[512,1024]{1,0:T(8,128)(2,1)S(1)}, u32[]{:S(2)}, u32[]{:S(2)}) collective-permute-start(bf16[512,1024]{1,0:T(8,128)(2,1)} %project.2), channel_id=1, source_target_pairs={{0,4},{4,0},{1,5},{5,1},{2,6},{6,2},{3,7},{7,3},{8,12},{12,8},{9,1... | collective-permute-start | bytes 3145736 | tf_op jit(solution)/shard_map/ppermute | solution.py:35
  216.4 1.1 copy-start.16
Sparse Core Ops, SparseCore 0:
  76.9 52.6 all-gather.6
  131.3 58.7 all-gather.4
